TPU v7x, 256 devices: a whole 4x4x8 slice. The times are simulated.
256 devices in a mesh: sub: 32 (over z, x), agg: 8 (over y, core).
Axes of the slice: x: 4, y: 4, z: 8, core: 2. Of those that a mesh axis runs over, the one named last changes fastest.
Arguments:
- dual_load: float32 [8, 32, 64, 1536], P('agg', 'sub'), may hold values from -58 to 58
- interface_inverse: bfloat16 [8, 32, 1536, 1536], P('agg', 'sub'), may hold values from -1 to 2.5, as said below
- dirichlet: bfloat16 [8, 32, 1536, 1536], P('agg', 'sub'), may hold values from -1 to 2.5, as said below
- coupling: bfloat16 [8, 32, 128, 1536], P('agg', 'sub'), may hold values from -0.15625 to 0.15625
- neighbours: int32 [8, 32, 8], P('agg', 'sub'), may hold values from -1 to 31, as said below
- face_counts: int32 [8, 32, 8], P('agg', 'sub'), may hold values from 0 to 192, as said below
- owners: int32 [8, 32, 128, 1], P('agg', 'sub'), may hold values from 0 to 7; in each aligned block of 128 rows (0 to 127, 128 to 255, ..., all dimensions but the last counted through in order) at most 48 rows name the same one
- primal_rows: int32 [8, 32, 128], P('agg', 'sub'), may hold values from 0 to 1023
- coarse_inverse: float32 [8, 1024, 1024], P('agg', 'sub'), may hold values from -1 to 1.5, as said below
Outputs:
- solution: float32 [8, 32, 64, 1536], P('agg', 'sub')
- residual: float32 [8, 32, 64, 1536], P('agg', 'sub')
Inputs may be any that keep to these rules, and one draw needn't show every extreme that they name: `neighbours`: each subdomain lists peers of its own aggregate by their index along sub, -1 in empty slots; no peer twice; if j lists i then i lists j; every listed peer lies within a cyclic distance of 4 along sub. `face_counts`: 0 exactly in empty slots, 48 or more elsewhere; both sides of a face give the same count and hold its rows in the same order. `owners`: among the 128 primal rows of one subdomain no aggregate is named more than 48 times. `interface_inverse`: each subdomain's matrix is symmetric positive definite. `dirichlet`: each subdomain's matrix is symmetric positive definite. `coarse_inverse`: each aggregate's matrix is symmetric positive definite.
All inputs are finite; a program needn't handle non-finite values.
Results may differ from a plain program's by a relative error of at most 0.011.
Values sent between devices are 32-bit elements; how exact they have to be, the bound alone decides.
No kernel may reach another device: no remote copies, remote signals or barrier semaphores. Data moves between devices by JAX's collectives and lax.ppermute only.
A program may use at most 128 MiB of HBM per device.

v0:
```python
import jax
import jax.numpy as jnp
from jax import lax
from jax.sharding import PartitionSpec as P

NC = 1024
CAP = 48
ITERS = 2
FULL_PRECISION = lax.Precision.HIGHEST
CONTRACT_LAST = (((1,), (1,)), ((), ()))


def from_behind_2(block, axis, distance):
    devices = range(lax.axis_size(axis))
    route = [((i - distance) % len(devices), i) for i in devices]
    return lax.ppermute(block, axis, route)


def shards(
    dual_load,
    interface_inverse,
    dirichlet,
    coupling,
    neighbours,
    face_counts,
    owners,
    primal_rows,
    coarse_inverse,
):
    inverse_block = interface_inverse[0, 0]
    dirichlet_block = dirichlet[0, 0]
    coupling_block = coupling[0, 0]
    peer_list = neighbours[0, 0]
    count_list = face_counts[0, 0]
    sub_count = lax.axis_size("sub")
    agg_count = lax.axis_size("agg")
    position = lax.axis_index("sub")
    slot_count = peer_list.shape[0]
    inner_order = inverse_block.shape[0]
    face_depth = inner_order // slot_count
    reach = min(4, (sub_count - 1) // 2)
    inside = (
        (jnp.arange(face_depth, dtype=jnp.int32)[None, :] < count_list[:, None])
        .reshape(1, inner_order)
        .astype(jnp.float32)
    )

    def assemble(local):
        case_count = local.shape[0]
        faces = local.reshape(case_count, slot_count, face_depth)
        placed = jnp.zeros_like(faces)
        for distance in range(1, reach + 1):
            ahead = (position + distance) % sub_count
            behind = (position + sub_count - distance) % sub_count
            to_ahead = (peer_list == ahead).astype(jnp.float32)[None, :, None]
            to_behind = (peer_list == behind).astype(jnp.float32)[None, :, None]
            upward = jnp.sum(faces * to_ahead, axis=1)
            downward = jnp.sum(faces * to_behind, axis=1)
            from_behind = from_behind_2(upward, "sub", distance)
            from_ahead = from_behind_2(downward, "sub", -distance)
            placed = (
                placed + to_behind * from_behind[:, None, :] + to_ahead * from_ahead[:, None, :]
            )
        return inside * (local + placed.reshape(case_count, inner_order))

    owner_ids = owners[0, 0, :, 0]
    row_ids = primal_rows[0, 0]
    owner_hot = (owner_ids[:, None] == jnp.arange(agg_count, dtype=jnp.int32)[None, :]).astype(
        jnp.int32
    )
    earlier = jnp.cumsum(owner_hot, axis=0) - owner_hot
    owner_rank = jnp.sum(earlier * owner_hot, axis=1)
    slot_index = owner_ids * CAP + owner_rank
    packing = slot_index[:, None] == jnp.arange(agg_count * CAP, dtype=jnp.int32)[None, :]
    packing_float = packing.astype(jnp.float32)
    sent_rows = jnp.sum(packing.astype(jnp.int32) * (row_ids[:, None] + 1), axis=0) - 1
    got_rows = lax.all_to_all(sent_rows, "agg", split_axis=0, concat_axis=0, tiled=True)
    scatter_hot = (got_rows[:, None] == jnp.arange(NC, dtype=jnp.int32)[None, :]).astype(
        jnp.float32
    )
    inverse_rows = coarse_inverse[0]

    def precondition(field):
        packed = field.astype(jnp.bfloat16)
        return assemble(
            inside * jnp.dot(packed, dirichlet_block, preferred_element_type=jnp.float32)
        )

    def residual_norm(first, second):
        return lax.psum(jnp.sum(first * second, axis=1), ("sub", "agg"))

    rhs = assemble(inside * dual_load[0, 0])
    solution = jnp.zeros_like(rhs)
    residual = rhs
    precond = precondition(residual)
    direction = precond
    residual_dot = residual_norm(residual, precond)
    for iteration in range(ITERS):
        operator_packed = direction.astype(jnp.bfloat16)
        own = jnp.dot(operator_packed, inverse_block, preferred_element_type=jnp.float32)
        terms = lax.dot_general(
            operator_packed, coupling_block, CONTRACT_LAST, preferred_element_type=jnp.float32
        )
        outgoing = jnp.dot(terms, packing_float, precision=FULL_PRECISION)
        gathered = jnp.dot(
            lax.all_to_all(outgoing, "agg", split_axis=1, concat_axis=1, tiled=True),
            scatter_hot,
            precision=FULL_PRECISION,
        )
        coarse_rhs = lax.psum(gathered, "sub")
        partial_rows = lax.dot_general(
            coarse_rhs, inverse_rows, CONTRACT_LAST, precision=FULL_PRECISION
        )
        coarse_sol = lax.all_gather(partial_rows, "sub", axis=1, tiled=True)
        answer = lax.dot_general(coarse_sol, scatter_hot, CONTRACT_LAST, precision=FULL_PRECISION)
        returned = lax.all_to_all(answer, "agg", split_axis=1, concat_axis=1, tiled=True)
        local_back = lax.dot_general(
            returned, packing_float, CONTRACT_LAST, precision=FULL_PRECISION
        )
        correction = jnp.dot(
            local_back.astype(jnp.bfloat16), coupling_block, preferred_element_type=jnp.float32
        )
        image = assemble(inside * (own + correction))
        alpha = (residual_dot / lax.psum(jnp.sum(direction * image, axis=1), ("sub", "agg")))[
            :, None
        ]
        solution = solution + alpha * direction
        residual = residual - alpha * image
        if iteration + 1 < ITERS:
            precond = precondition(residual)
            next_dot = residual_norm(residual, precond)
            direction = precond + (next_dot / residual_dot)[:, None] * direction
            residual_dot = next_dot
    return (solution[None, None], residual[None, None])


def solution(mesh):
    in_specs = (
        P("agg", "sub", None, None),
        P("agg", "sub", None, None),
        P("agg", "sub", None, None),
        P("agg", "sub", None, None),
        P("agg", "sub", None),
        P("agg", "sub", None),
        P("agg", "sub", None, None),
        P("agg", "sub", None),
        P("agg", "sub", None),
    )
    out_specs = (P("agg", "sub", None, None), P("agg", "sub", None, None))
    return jax.shard_map(shards, mesh=mesh, in_specs=in_specs, out_specs=out_specs, check_vma=False)
```

profile of v0, /device:TPU:1, one launch (start us, length us, event | category | flops | bytes accessed | tf_op | source)
XLA Modules:
  0.0 917.8 jit_solution(6425770265424465426)
XLA Ops:
  13.6 6.6 collective-permute-start.1
  20.4 2.7 collective-permute-start.7
  28.4 2.6 collective-permute-start.3
  50.8 5.2 fusion.8
  58.0 2.5 multiply_reduce_fusion.31
  60.5 4.7 collective-permute-start.11
  65.2 2.7 collective-permute-start.9
  76.5 10.1 %all-to-all-start.1 = ((s32[8,48,1]{1,2,0:T(1,128)}), s32[8,48,1]{1,2,0:T(1,128)}, u32[]{:S(2)}, u32[]{:S(2)}) async-start(s32[8,48,1]{1,2,0:T(1,128)} %bitcast.111), calls=%async_computation.1 | async-start | bytes 8192 | tf_op jit(solution)/shard_map/all_to_all | solution.py:77
  119.4 4.8 all-to-all-start
  136.4 138.3 %all-reduce.4.cloned.1.call-done = f32[64,1024]{1,0:T(8,128)} async-done(((f32[64,1024]{1,0:T(8,128)}), f32[64,1024]{1,0:T(8,128)}) %all-reduce.4.cloned.1.call-update) | async-done | bytes 262160 | tf_op jit(solution)/shard_map/psum | solution.py:110
  275.9 35.9 %all_gather.6 = f32[64,1024]{0,1:T(8,128)S(1)} all-gather(f32[64,32]{0,1:T(8,128)S(1)} %fusion.58), channel_id=1, replica_groups=mesh['sub'=32,'agg'=8] {'sub'}, dimensions={1}, use_global_device_ids=true | all-gather | bytes 270336 | tf_op jit(solution)/shard_map/all_gather | solution.py:114
  315.8 26.7 %all_to_all.54 = f32[8,1,3072]{2,1,0:T(1,128)} all-to-all(f32[8,1,3072]{2,1,0:T(1,128)} %reshape.670), channel_id=1, replica_groups=mesh['sub'=32,'agg'=8] {'agg'}, dimensions={0} | all-to-all | bytes 196608 | tf_op jit(solution)/shard_map/all_to_all | solution.py:116
  348.1 4.0 fusion.23
  354.1 3.2 multiply_reduce_fusion.23
  360.2 4.5 collective-permute-start.17
  364.7 3.8 collective-permute-start.21
  368.5 2.7 collective-permute-start.23
  394.4 3.9 multiply_reduce_fusion.42
  398.5 77.6 %all-reduce = (f32[64]{0:T(128)S(1)}, f32[64]{0:T(128)S(1)}) all-reduce(f32[64]{0:T(128)S(1)} %get-tuple-element.43, f32[64]{0:T(128)S(1)} %get-tuple-element.42), channel_id=1, replica_groups=mesh['sub'=32,'agg'=8] {'sub','agg'}, use_global_device_ids=true, to_apply=%region_17.18 | all-reduce | flops 128 | bytes 1024 | tf_op jit(solution)/shard_map/psum | solution.py:90
  477.2 3.3 fusion.11
  488.2 3.5 collective-permute-start.29
  491.7 2.7 collective-permute-start.31
  505.9 77.6 %psum.45 = f32[64]{0:T(128)S(1)} all-reduce(f32[64]{0:T(128)S(1)} %get-tuple-element.48), channel_id=1, replica_groups=mesh['sub'=32,'agg'=8] {'sub','agg'}, use_global_device_ids=true, to_apply=%region_41.42 | all-reduce | flops 64 | bytes 512 | tf_op jit(solution)/shard_map/psum | solution.py:90
  585.7 8.1 all_to_all.55
  596.3 136.3 %all-reduce.6.cloned.1.call-done = f32[64,1024]{1,0:T(8,128)} async-done(((f32[64,1024]{1,0:T(8,128)}), f32[64,1024]{1,0:T(8,128)}) %all-reduce.6.cloned.1.call-update) | async-done | bytes 262160 | tf_op jit(solution)/shard_map/psum | solution.py:110
  733.9 35.9 %all_gather.7 = f32[64,1024]{0,1:T(8,128)S(1)} all-gather(f32[64,32]{0,1:T(8,128)S(1)} %fusion.56), channel_id=1, replica_groups=mesh['sub'=32,'agg'=8] {'sub'}, dimensions={1}, use_global_device_ids=true | all-gather | bytes 270336 | tf_op jit(solution)/shard_map/all_gather | solution.py:114
  770.8 26.7 %all_to_all.56 = f32[8,1,3072]{2,1,0:T(1,128)S(1)} all-to-all(f32[8,1,3072]{2,1,0:T(1,128)S(1)} %reshape.674), channel_id=1, replica_groups=mesh['sub'=32,'agg'=8] {'agg'}, dimensions={0} | all-to-all | bytes 196608 | tf_op jit(solution)/shard_map/all_to_all | solution.py:116
  799.1 3.3 fusion.20
  807.2 4.5 collective-permute-start.33
  811.7 3.6 collective-permute-start.37
  815.3 2.7 collective-permute-start.39
  831.3 77.7 %psum.47 = f32[64]{0:T(128)S(1)} all-reduce(f32[64]{0:T(128)S(1)} %get-tuple-element.46), channel_id=1, replica_groups=mesh['sub'=32,'agg'=8] {'sub','agg'}, use_global_device_ids=true, to_apply=%region_52.53 | all-reduce | flops 64 | bytes 512 | tf_op jit(solution)/shard_map/psum | solution.py:124
  (347 shorter events, 174.0 us)
Async XLA Ops:
  11.5 35.6 %collective-permute-start = (f32[64,192]{1,0:T(8,128)S(1)}, f32[64,192]{1,0:T(8,128)}, u32[]{:S(2)}, u32[]{:S(2)}) collective-permute-start(f32[64,192]{1,0:T(8,128)S(1)} %get-tuple-element.2), channel_id=1, source_target_pairs={{248,0},{0,8},{8,16},{16,24},{24,32},{32,40},{40,48},{48,56},{56,6... | collective-permute-start | bytes 147464 | tf_op jit(solution)/shard_map/ppermute | solution.py:16
  13.6 29.9 %collective-permute-start.1 = (f32[64,192]{1,0:T(8,128)}, f32[64,192]{1,0:T(8,128)}, u32[]{:S(2)}, u32[]{:S(2)}) collective-permute-start(f32[64,192]{1,0:T(8,128)} %get-tuple-element.3), channel_id=1, source_target_pairs={{8,0},{16,8},{24,16},{32,24},{40,32},{48,40},{56,48},{64,56},{72,6... | collective-permute-start | bytes 147464 | tf_op jit(solution)/shard_map/ppermute | solution.py:16
  20.4 10.7 %collective-permute-start.7 = (f32[64,192]{1,0:T(8,128)S(1)}, f32[64,192]{1,0:T(8,128)S(1)}, u32[]{:S(2)}, u32[]{:S(2)}) collective-permute-start(f32[64,192]{1,0:T(8,128)S(1)} %get-tuple-element.9), channel_id=1, source_target_pairs={{32,0},{40,8},{48,16},{56,24},{64,32},{72,40},{80,48},{88,56},{96,... | collective-permute-start | bytes 147464 | tf_op jit(solution)/shard_map/ppermute | solution.py:16
  26.0 13.9 %collective-permute-start.2 = (f32[64,192]{1,0:T(8,128)}, f32[64,192]{1,0:T(8,128)}, u32[]{:S(2)}, u32[]{:S(2)}) collective-permute-start(f32[64,192]{1,0:T(8,128)} %get-tuple-element.4), channel_id=1, source_target_pairs={{240,0},{248,8},{0,16},{8,24},{16,32},{24,40},{32,48},{40,56},{48,... | collective-permute-start | bytes 147464 | tf_op jit(solution)/shard_map/ppermute | solution.py:16
  28.4 9.6 %collective-permute-start.3 = (f32[64,192]{1,0:T(8,128)S(1)}, f32[64,192]{1,0:T(8,128)}, u32[]{:S(2)}, u32[]{:S(2)}) collective-permute-start(f32[64,192]{1,0:T(8,128)S(1)} %get-tuple-element.5), channel_id=1, source_target_pairs={{16,0},{24,8},{32,16},{40,24},{48,32},{56,40},{64,48},{72,56},{80,... | collective-permute-start | bytes 147464 | tf_op jit(solution)/shard_map/ppermute | solution.py:16
  68.6 41.9 %collective-permute-start.8 = (f32[64,192]{1,0:T(8,128)S(1)}, f32[64,192]{1,0:T(8,128)S(1)}, u32[]{:S(2)}, u32[]{:S(2)}) collective-permute-start(f32[64,192]{1,0:T(8,128)S(1)} %get-tuple-element.34), channel_id=1, source_target_pairs={{248,0},{0,8},{8,16},{16,24},{24,32},{32,40},{40,48},{48,56},{56,6... | collective-permute-start | bytes 147464 | tf_op jit(solution)/shard_map/ppermute | solution.py:16
  68.7 39.0 %collective-permute-start.15 = (f32[64,192]{1,0:T(8,128)S(1)}, f32[64,192]{1,0:T(8,128)S(1)}, u32[]{:S(2)}, u32[]{:S(2)}) collective-permute-start(f32[64,192]{1,0:T(8,128)S(1)} %get-tuple-element.35), channel_id=1, source_target_pairs={{32,0},{40,8},{48,16},{56,24},{64,32},{72,40},{80,48},{88,56},{96,... | collective-permute-start | bytes 147464 | tf_op jit(solution)/shard_map/ppermute | solution.py:16
  68.8 35.2 %collective-permute-start.14 = (f32[64,192]{1,0:T(8,128)S(1)}, f32[64,192]{1,0:T(8,128)}, u32[]{:S(2)}, u32[]{:S(2)}) collective-permute-start(f32[64,192]{1,0:T(8,128)S(1)} %get-tuple-element.36), channel_id=1, source_target_pairs={{224,0},{232,8},{240,16},{248,24},{0,32},{8,40},{16,48},{24,56},{3... | collective-permute-start | bytes 147464 | tf_op jit(solution)/shard_map/ppermute | solution.py:16
  71.9 28.5 %collective-permute-start.13 = (f32[64,192]{1,0:T(8,128)S(1)}, f32[64,192]{1,0:T(8,128)}, u32[]{:S(2)}, u32[]{:S(2)}) collective-permute-start(f32[64,192]{1,0:T(8,128)S(1)} %get-tuple-element.37), channel_id=1, source_target_pairs={{24,0},{32,8},{40,16},{48,24},{56,32},{64,40},{72,48},{80,56},{88,... | collective-permute-start | bytes 147464 | tf_op jit(solution)/shard_map/ppermute | solution.py:16
  73.5 23.3 %collective-permute-start.12 = (f32[64,192]{1,0:T(8,128)S(1)}, f32[64,192]{1,0:T(8,128)}, u32[]{:S(2)}, u32[]{:S(2)}) collective-permute-start(f32[64,192]{1,0:T(8,128)S(1)} %get-tuple-element.38), channel_id=1, source_target_pairs={{232,0},{240,8},{248,16},{0,24},{8,32},{16,40},{24,48},{32,56},{40... | collective-permute-start | bytes 147464 | tf_op jit(solution)/shard_map/ppermute | solution.py:16
  76.5 42.9 %all-to-all-start.1 = ((s32[8,48,1]{1,2,0:T(1,128)}), s32[8,48,1]{1,2,0:T(1,128)}, u32[]{:S(2)}, u32[]{:S(2)}) async-start(s32[8,48,1]{1,2,0:T(1,128)} %bitcast.111), calls=%async_computation.1 | async-start | bytes 8192 | tf_op jit(solution)/shard_map/all_to_all | solution.py:77
  119.4 9.9 %all-to-all-start = ((f32[8,1,3072]{2,1,0:T(1,128)}), f32[8,1,3072]{2,1,0:T(1,128)}, u32[]{:S(2)}, u32[]{:S(2)}) async-start(f32[8,1,3072]{2,1,0:T(1,128)} %reshape.668), calls=%async_computation | async-start | bytes 196608 | tf_op jit(solution)/shard_map/all_to_all | solution.py:106
  124.2 150.4 %all-reduce.4.cloned.1.call-start = ((), (), s32[]{:S(2)}) async-start(), calls=%async_computation.5 | async-start | bytes 524288 | tf_op jit(solution)/shard_map/psum | solution.py:110
  136.3 596.3 %all-reduce.6.cloned.1.call-start = ((), (), s32[]{:S(2)}) async-start(), calls=%async_computation.6 | async-start | bytes 524288 | tf_op jit(solution)/shard_map/psum | solution.py:110
  357.3 11.3 %collective-permute-start.19 = (f32[64,192]{1,0:T(8,128)S(1)}, f32[64,192]{1,0:T(8,128)}, u32[]{:S(2)}, u32[]{:S(2)}) collective-permute-start(f32[64,192]{1,0:T(8,128)S(1)} %get-tuple-element.31), channel_id=1, source_target_pairs={{16,0},{24,8},{32,16},{40,24},{48,32},{56,40},{64,48},{72,56},{80,... | collective-permute-start | bytes 147464 | tf_op jit(solution)/shard_map/ppermute | solution.py:16
  359.2 9.3 %collective-permute-start.18 = (f32[64,192]{1,0:T(8,128)S(1)}, f32[64,192]{1,0:T(8,128)}, u32[]{:S(2)}, u32[]{:S(2)}) collective-permute-start(f32[64,192]{1,0:T(8,128)S(1)} %get-tuple-element.32), channel_id=1, source_target_pairs={{240,0},{248,8},{0,16},{8,24},{16,32},{24,40},{32,48},{40,56},{48,... | collective-permute-start | bytes 147464 | tf_op jit(solution)/shard_map/ppermute | solution.py:16
  360.2 11.0 %collective-permute-start.17 = (f32[64,192]{1,0:T(8,128)S(1)}, f32[64,192]{1,0:T(8,128)}, u32[]{:S(2)}, u32[]{:S(2)}) collective-permute-start(f32[64,192]{1,0:T(8,128)S(1)} %get-tuple-element.33), channel_id=1, source_target_pairs={{8,0},{16,8},{24,16},{32,24},{40,32},{48,40},{56,48},{64,56},{72,6... | collective-permute-start | bytes 147464 | tf_op jit(solution)/shard_map/ppermute | solution.py:16
  364.7 20.5 %collective-permute-start.20 = (f32[64,192]{1,0:T(8,128)}, f32[64,192]{1,0:T(8,128)}, u32[]{:S(2)}, u32[]{:S(2)}) collective-permute-start(f32[64,192]{1,0:T(8,128)} %get-tuple-element.30), channel_id=1, source_target_pairs={{232,0},{240,8},{248,16},{0,24},{8,32},{16,40},{24,48},{32,56},{40... | collective-permute-start | bytes 147464 | tf_op jit(solution)/shard_map/ppermute | solution.py:16
  364.7 22.3 %collective-permute-start.21 = (f32[64,192]{1,0:T(8,128)}, f32[64,192]{1,0:T(8,128)}, u32[]{:S(2)}, u32[]{:S(2)}) collective-permute-start(f32[64,192]{1,0:T(8,128)} %get-tuple-element.29), channel_id=1, source_target_pairs={{24,0},{32,8},{40,16},{48,24},{56,32},{64,40},{72,48},{80,56},{88,... | collective-permute-start | bytes 147464 | tf_op jit(solution)/shard_map/ppermute | solution.py:16
  368.5 20.4 %collective-permute-start.22 = (f32[64,192]{1,0:T(8,128)}, f32[64,192]{1,0:T(8,128)}, u32[]{:S(2)}, u32[]{:S(2)}) collective-permute-start(f32[64,192]{1,0:T(8,128)} %get-tuple-element.28), channel_id=1, source_target_pairs={{224,0},{232,8},{240,16},{248,24},{0,32},{8,40},{16,48},{24,56},{3... | collective-permute-start | bytes 147464 | tf_op jit(solution)/shard_map/ppermute | solution.py:16
  368.5 22.2 %collective-permute-start.23 = (f32[64,192]{1,0:T(8,128)}, f32[64,192]{1,0:T(8,128)}, u32[]{:S(2)}, u32[]{:S(2)}) collective-permute-start(f32[64,192]{1,0:T(8,128)} %get-tuple-element.27), channel_id=1, source_target_pairs={{32,0},{40,8},{48,16},{56,24},{64,32},{72,40},{80,48},{88,56},{96,... | collective-permute-start | bytes 147464 | tf_op jit(solution)/shard_map/ppermute | solution.py:16
  371.2 21.3 %collective-permute-start.16 = (f32[64,192]{1,0:T(8,128)}, f32[64,192]{1,0:T(8,128)}, u32[]{:S(2)}, u32[]{:S(2)}) collective-permute-start(f32[64,192]{1,0:T(8,128)} %get-tuple-element.26), channel_id=1, source_target_pairs={{248,0},{0,8},{8,16},{16,24},{24,32},{32,40},{40,48},{48,56},{56,6... | collective-permute-start | bytes 147464 | tf_op jit(solution)/shard_map/ppermute | solution.py:16
  482.7 9.0 collective-permute-start.27
  485.6 8.7 collective-permute-start.25
  488.2 8.7 collective-permute-start.29
  491.7 8.8 collective-permute-start.31
  804.3 11.0 %collective-permute-start.35 = (f32[64,192]{1,0:T(8,128)S(1)}, f32[64,192]{1,0:T(8,128)S(1)}, u32[]{:S(2)}, u32[]{:S(2)}) collective-permute-start(f32[64,192]{1,0:T(8,128)S(1)} %get-tuple-element.15), channel_id=1, source_target_pairs={{16,0},{24,8},{32,16},{40,24},{48,32},{56,40},{64,48},{72,56},{80,... | collective-permute-start | bytes 147464 | tf_op jit(solution)/shard_map/ppermute | solution.py:16
  806.2 9.1 collective-permute-start.34
  807.2 10.8 %collective-permute-start.33 = (f32[64,192]{1,0:T(8,128)S(1)}, f32[64,192]{1,0:T(8,128)S(1)}, u32[]{:S(2)}, u32[]{:S(2)}) collective-permute-start(f32[64,192]{1,0:T(8,128)S(1)} %get-tuple-element.17), channel_id=1, source_target_pairs={{8,0},{16,8},{24,16},{32,24},{40,32},{48,40},{56,48},{64,56},{72,6... | collective-permute-start | bytes 147464 | tf_op jit(solution)/shard_map/ppermute | solution.py:16
  811.7 10.3 %collective-permute-start.37 = (f32[64,192]{1,0:T(8,128)}, f32[64,192]{1,0:T(8,128)}, u32[]{:S(2)}, u32[]{:S(2)}) collective-permute-start(f32[64,192]{1,0:T(8,128)} %get-tuple-element.13), channel_id=1, source_target_pairs={{24,0},{32,8},{40,16},{48,24},{56,32},{64,40},{72,48},{80,56},{88,... | collective-permute-start | bytes 147464 | tf_op jit(solution)/shard_map/ppermute | solution.py:16
  815.3 10.3 %collective-permute-start.39 = (f32[64,192]{1,0:T(8,128)S(1)}, f32[64,192]{1,0:T(8,128)}, u32[]{:S(2)}, u32[]{:S(2)}) collective-permute-start(f32[64,192]{1,0:T(8,128)S(1)} %get-tuple-element.11), channel_id=1, source_target_pairs={{32,0},{40,8},{48,16},{56,24},{64,32},{72,40},{80,48},{88,56},{96,... | collective-permute-start | bytes 147464 | tf_op jit(solution)/shard_map/ppermute | solution.py:16
  818.0 9.5 %collective-permute-start.32 = (f32[64,192]{1,0:T(8,128)S(1)}, f32[64,192]{1,0:T(8,128)}, u32[]{:S(2)}, u32[]{:S(2)}) collective-permute-start(f32[64,192]{1,0:T(8,128)S(1)} %get-tuple-element.10), channel_id=1, source_target_pairs={{248,0},{0,8},{8,16},{16,24},{24,32},{32,40},{40,48},{48,56},{56,6... | collective-permute-start | bytes 147464 | tf_op jit(solution)/shard_map/ppermute | solution.py:16
  (68 other events, 2431.6 us)
Sparse Core Ops, SparseCore 0:
  136.4 138.1 all-reduce.3
  596.4 136.1 all-reduce.5
where the time goes:
time: 927 us; the launch traced here: 918 us
  blocking collectives  366 us (39%)
  waiting for transfers between devices  278 us (30%)
  local copies, waits for them, and re-layouts  105 us (11%)
  starting transfers between devices  83.3 us (9%)
  other arithmetic  39.7 us (4%)
  matrix products  30.5 us (3%)
  between operations  15.6 us (2%)
    psum x2, waiting for transfers between devices, shards(): coarse_rhs = lax.psum(gathered, 'sub')  275 us
    psum x2, blocking collectives, residual_norm(): return lax.psum(jnp.sum(first * second, axis=1), ('sub', 'agg'))  155 us
    psum x1, blocking collectives, shards(): lax.psum(jnp.sum(direction * image, axis=1), ('sub', 'agg'))  77.7 us
    all_gather x2, blocking collectives, shards(): coarse_sol = lax.all_gather(partial_rows, 'sub', axis=1, tiled=True)  71.7 us
    ppermute x40, starting transfers between devices, from_behind_2(): return lax.ppermute(block, axis, route)  68.3 us
    all_to_all x2, blocking collectives, shards(): lax.all_to_all(answer, 'agg', split_axis=1, concat_axis=1, tiled=True)  53.4 us
    mul x52, local copies, waits for them, and re-layouts, assemble(): to_behind * from_behind[:, None, :]  46.7 us
    mul x44, local copies, waits for them, and re-layouts, assemble(): to_ahead * from_ahead[:, None, :]  40.9 us
  transfers between devices with their start and end apart: 44, of which 4 were waited for; matrix products, arithmetic and copies ran while one was open for 10% of the time, Pallas kernels for 0%

commit v1 on v0

--- a/solution.py
+++ b/solution.py
@@ -111,7 +111,9 @@
         partial_rows = lax.dot_general(
             coarse_rhs, inverse_rows, CONTRACT_LAST, precision=FULL_PRECISION
         )
-        coarse_sol = lax.all_gather(partial_rows, "sub", axis=1, tiled=True)
+        coarse_sol = jnp.concatenate(
+            lax.all_to_all(jnp.stack([partial_rows] * lax.axis_size("sub")), "sub", 0, 0), axis=1
+        )
         answer = lax.dot_general(coarse_sol, scatter_hot, CONTRACT_LAST, precision=FULL_PRECISION)
         returned = lax.all_to_all(answer, "agg", split_axis=1, concat_axis=1, tiled=True)
         local_back = lax.dot_general(

time: 927 us -> 873 us (0.942)
  blocking collectives: 366 us -> 304 us
    all_gather x2 -> x0, blocking collectives: 71.7 us -> none  [shards(): coarse_sol = lax.all_gather(partial_rows, 'sub', axis=1, tiled=True)]
    all_to_all x0 -> x2, blocking collectives: none -> 30.6 us  [shards(): lax.all_to_all(jnp.stack([partial_rows] * lax.axis_size('sub')), 'sub', 0...]
    all_to_all x2, blocking collectives: 53.4 us -> 32.5 us  [shards(): lax.all_to_all(answer, 'agg', split_axis=1, concat_axis=1, tiled=True)]
  transfers between devices with their start and end apart: 44 -> 44, of which waited for: 4 -> 4; matrix products, arithmetic and copies ran while one was open for 10% -> 11% of each run, Pallas kernels for 0% -> 0%
where the time goes in v1:
time: 873 us; the launch traced here: 863 us
  blocking collectives  304 us (35%)
  waiting for transfers between devices  278 us (32%)
  local copies, waits for them, and re-layouts  110 us (13%)
  starting transfers between devices  79.8 us (9%)
  other arithmetic  43.4 us (5%)
  matrix products  31.6 us (4%)
  between operations  15.4 us (2%)
    psum x2, waiting for transfers between devices, shards(): coarse_rhs = lax.psum(gathered, 'sub')  275 us
    psum x2, blocking collectives, residual_norm(): return lax.psum(jnp.sum(first * second, axis=1), ('sub', 'agg'))  155 us
    psum x1, blocking collectives, shards(): lax.psum(jnp.sum(direction * image, axis=1), ('sub', 'agg'))  77.8 us
    ppermute x40, starting transfers between devices, from_behind_2(): return lax.ppermute(block, axis, route)  64.7 us
    mul x52, local copies, waits for them, and re-layouts, assemble(): to_behind * from_behind[:, None, :]  46.7 us
    mul x44, local copies, waits for them, and re-layouts, assemble(): to_ahead * from_ahead[:, None, :]  40.9 us
    all_to_all x2, blocking collectives, shards(): lax.all_to_all(answer, 'agg', split_axis=1, concat_axis=1, tiled=True)  32.5 us
    all_to_all x2, blocking collectives, shards(): lax.all_to_all(jnp.stack([partial_rows] * lax.axis_size('sub')), 'sub', 0...  30.6 us
  transfers between devices with their start and end apart: 44, of which 4 were waited for; matrix products, arithmetic and copies ran while one was open for 11% of the time, Pallas kernels for 0%

profile of v1, /device:TPU:1, one launch (start us, length us, event | category | flops | bytes accessed | tf_op | source)
XLA Modules:
  0.0 863.3 jit_solution(11759537969766863169)
XLA Ops:
  13.6 6.6 collective-permute-start.1
  20.4 2.7 collective-permute-start.7
  28.4 2.6 collective-permute-start.3
  50.9 5.2 fusion.8
  60.6 4.7 collective-permute-start.11
  65.3 2.7 collective-permute-start.9
  76.7 10.3 %all-to-all-start.1 = ((s32[8,48,1]{1,2,0:T(1,128)}), s32[8,48,1]{1,2,0:T(1,128)}, u32[]{:S(2)}, u32[]{:S(2)}) async-start(s32[8,48,1]{1,2,0:T(1,128)} %sub.24), calls=%async_computation.1 | async-start | bytes 8192 | tf_op jit(solution)/shard_map/all_to_all | solution.py:77
  119.7 4.8 all-to-all-start
  136.5 138.2 %all-reduce.4.cloned.1.call-done = f32[64,1024]{1,0:T(8,128)} async-done(((f32[64,1024]{1,0:T(8,128)}), f32[64,1024]{1,0:T(8,128)}) %all-reduce.4.cloned.1.call-update) | async-done | bytes 262160 | tf_op jit(solution)/shard_map/psum | solution.py:110
  279.0 15.2 %all_to_all.61 = f32[32,1,2048]{2,1,0:T(1,128)} all-to-all(f32[32,1,2048]{2,1,0:T(1,128)} %reshape.727), channel_id=1, replica_groups=mesh['sub'=32,'agg'=8] {'sub'}, dimensions={0} | all-to-all | bytes 524288 | tf_op jit(solution)/shard_map/all_to_all | solution.py:115
  294.2 2.8 reduce.5
  299.0 2.6 fusion.82
  303.3 16.4 %all_to_all.62 = f32[8,1,3072]{2,1,0:T(1,128)} all-to-all(f32[8,1,3072]{2,1,0:T(1,128)} %reshape.729), channel_id=1, replica_groups=mesh['sub'=32,'agg'=8] {'agg'}, dimensions={0} | all-to-all | bytes 196608 | tf_op jit(solution)/shard_map/all_to_all | solution.py:118
  325.2 4.0 fusion.23
  331.2 3.2 multiply_reduce_fusion.23
  337.4 2.8 collective-permute-start.17
  340.1 3.6 collective-permute-start.21
  343.7 2.7 collective-permute-start.23
  369.6 3.9 multiply_reduce_fusion.42
  373.6 77.8 %all-reduce = (f32[64]{0:T(128)S(1)}, f32[64]{0:T(128)S(1)}) all-reduce(f32[64]{0:T(128)S(1)} %get-tuple-element.43, f32[64]{0:T(128)S(1)} %get-tuple-element.42), channel_id=1, replica_groups=mesh['sub'=32,'agg'=8] {'sub','agg'}, use_global_device_ids=true, to_apply=%region_17.18 | all-reduce | flops 128 | bytes 1024 | tf_op jit(solution)/shard_map/psum | solution.py:90
  452.5 3.2 fusion.11
  463.5 3.5 collective-permute-start.29
  467.0 2.7 collective-permute-start.31
  481.2 77.6 %psum.45 = f32[64]{0:T(128)S(1)} all-reduce(f32[64]{0:T(128)S(1)} %get-tuple-element.48), channel_id=1, replica_groups=mesh['sub'=32,'agg'=8] {'sub','agg'}, use_global_device_ids=true, to_apply=%region_41.42 | all-reduce | flops 64 | bytes 512 | tf_op jit(solution)/shard_map/psum | solution.py:90
  561.1 8.1 all_to_all.63
  571.6 137.1 %all-reduce.6.cloned.1.call-done = f32[64,1024]{1,0:T(8,128)} async-done(((f32[64,1024]{1,0:T(8,128)}), f32[64,1024]{1,0:T(8,128)}) %all-reduce.6.cloned.1.call-update) | async-done | bytes 262160 | tf_op jit(solution)/shard_map/psum | solution.py:110
  710.4 15.4 %all_to_all.64 = f32[32,1,2048]{2,1,0:T(1,128)S(1)} all-to-all(f32[32,1,2048]{2,1,0:T(1,128)S(1)} %reshape.733), channel_id=1, replica_groups=mesh['sub'=32,'agg'=8] {'sub'}, dimensions={0} | all-to-all | bytes 524288 | tf_op jit(solution)/shard_map/all_to_all | solution.py:115
  728.9 16.1 %all_to_all.65 = f32[8,1,3072]{2,1,0:T(1,128)S(1)} all-to-all(f32[8,1,3072]{2,1,0:T(1,128)S(1)} %reshape.735), channel_id=1, replica_groups=mesh['sub'=32,'agg'=8] {'agg'}, dimensions={0} | all-to-all | bytes 196608 | tf_op jit(solution)/shard_map/all_to_all | solution.py:118
  746.4 3.3 fusion.20
  757.2 3.6 collective-permute-start.37
  760.8 2.7 collective-permute-start.39
  776.9 77.8 %psum.47 = f32[64]{0:T(128)S(1)} all-reduce(f32[64]{0:T(128)S(1)} %get-tuple-element.46), channel_id=1, replica_groups=mesh['sub'=32,'agg'=8] {'sub','agg'}, use_global_device_ids=true, to_apply=%region_52.53 | all-reduce | flops 64 | bytes 512 | tf_op jit(solution)/shard_map/psum | solution.py:126
  (353 shorter events, 184.0 us)
Async XLA Ops:
  11.5 35.7 %collective-permute-start = (f32[64,192]{1,0:T(8,128)S(1)}, f32[64,192]{1,0:T(8,128)}, u32[]{:S(2)}, u32[]{:S(2)}) collective-permute-start(f32[64,192]{1,0:T(8,128)S(1)} %get-tuple-element.2), channel_id=1, source_target_pairs={{248,0},{0,8},{8,16},{16,24},{24,32},{32,40},{40,48},{48,56},{56,6... | collective-permute-start | bytes 147464 | tf_op jit(solution)/shard_map/ppermute | solution.py:16
  13.6 30.0 %collective-permute-start.1 = (f32[64,192]{1,0:T(8,128)}, f32[64,192]{1,0:T(8,128)}, u32[]{:S(2)}, u32[]{:S(2)}) collective-permute-start(f32[64,192]{1,0:T(8,128)} %get-tuple-element.3), channel_id=1, source_target_pairs={{8,0},{16,8},{24,16},{32,24},{40,32},{48,40},{56,48},{64,56},{72,6... | collective-permute-start | bytes 147464 | tf_op jit(solution)/shard_map/ppermute | solution.py:16
  20.4 10.7 %collective-permute-start.7 = (f32[64,192]{1,0:T(8,128)S(1)}, f32[64,192]{1,0:T(8,128)S(1)}, u32[]{:S(2)}, u32[]{:S(2)}) collective-permute-start(f32[64,192]{1,0:T(8,128)S(1)} %get-tuple-element.9), channel_id=1, source_target_pairs={{32,0},{40,8},{48,16},{56,24},{64,32},{72,40},{80,48},{88,56},{96,... | collective-permute-start | bytes 147464 | tf_op jit(solution)/shard_map/ppermute | solution.py:16
  26.0 14.0 %collective-permute-start.2 = (f32[64,192]{1,0:T(8,128)}, f32[64,192]{1,0:T(8,128)}, u32[]{:S(2)}, u32[]{:S(2)}) collective-permute-start(f32[64,192]{1,0:T(8,128)} %get-tuple-element.4), channel_id=1, source_target_pairs={{240,0},{248,8},{0,16},{8,24},{16,32},{24,40},{32,48},{40,56},{48,... | collective-permute-start | bytes 147464 | tf_op jit(solution)/shard_map/ppermute | solution.py:16
  28.4 9.7 %collective-permute-start.3 = (f32[64,192]{1,0:T(8,128)S(1)}, f32[64,192]{1,0:T(8,128)}, u32[]{:S(2)}, u32[]{:S(2)}) collective-permute-start(f32[64,192]{1,0:T(8,128)S(1)} %get-tuple-element.5), channel_id=1, source_target_pairs={{16,0},{24,8},{32,16},{40,24},{48,32},{56,40},{64,48},{72,56},{80,... | collective-permute-start | bytes 147464 | tf_op jit(solution)/shard_map/ppermute | solution.py:16
  68.8 42.1 %collective-permute-start.8 = (f32[64,192]{1,0:T(8,128)S(1)}, f32[64,192]{1,0:T(8,128)S(1)}, u32[]{:S(2)}, u32[]{:S(2)}) collective-permute-start(f32[64,192]{1,0:T(8,128)S(1)} %get-tuple-element.34), channel_id=1, source_target_pairs={{248,0},{0,8},{8,16},{16,24},{24,32},{32,40},{40,48},{48,56},{56,6... | collective-permute-start | bytes 147464 | tf_op jit(solution)/shard_map/ppermute | solution.py:16
  68.8 39.1 %collective-permute-start.15 = (f32[64,192]{1,0:T(8,128)S(1)}, f32[64,192]{1,0:T(8,128)S(1)}, u32[]{:S(2)}, u32[]{:S(2)}) collective-permute-start(f32[64,192]{1,0:T(8,128)S(1)} %get-tuple-element.35), channel_id=1, source_target_pairs={{32,0},{40,8},{48,16},{56,24},{64,32},{72,40},{80,48},{88,56},{96,... | collective-permute-start | bytes 147464 | tf_op jit(solution)/shard_map/ppermute | solution.py:16
  68.9 35.4 %collective-permute-start.14 = (f32[64,192]{1,0:T(8,128)S(1)}, f32[64,192]{1,0:T(8,128)}, u32[]{:S(2)}, u32[]{:S(2)}) collective-permute-start(f32[64,192]{1,0:T(8,128)S(1)} %get-tuple-element.36), channel_id=1, source_target_pairs={{224,0},{232,8},{240,16},{248,24},{0,32},{8,40},{16,48},{24,56},{3... | collective-permute-start | bytes 147464 | tf_op jit(solution)/shard_map/ppermute | solution.py:16
  72.0 28.7 %collective-permute-start.13 = (f32[64,192]{1,0:T(8,128)S(1)}, f32[64,192]{1,0:T(8,128)}, u32[]{:S(2)}, u32[]{:S(2)}) collective-permute-start(f32[64,192]{1,0:T(8,128)S(1)} %get-tuple-element.37), channel_id=1, source_target_pairs={{24,0},{32,8},{40,16},{48,24},{56,32},{64,40},{72,48},{80,56},{88,... | collective-permute-start | bytes 147464 | tf_op jit(solution)/shard_map/ppermute | solution.py:16
  73.6 23.5 %collective-permute-start.12 = (f32[64,192]{1,0:T(8,128)S(1)}, f32[64,192]{1,0:T(8,128)}, u32[]{:S(2)}, u32[]{:S(2)}) collective-permute-start(f32[64,192]{1,0:T(8,128)S(1)} %get-tuple-element.38), channel_id=1, source_target_pairs={{232,0},{240,8},{248,16},{0,24},{8,32},{16,40},{24,48},{32,56},{40... | collective-permute-start | bytes 147464 | tf_op jit(solution)/shard_map/ppermute | solution.py:16
  76.7 43.0 %all-to-all-start.1 = ((s32[8,48,1]{1,2,0:T(1,128)}), s32[8,48,1]{1,2,0:T(1,128)}, u32[]{:S(2)}, u32[]{:S(2)}) async-start(s32[8,48,1]{1,2,0:T(1,128)} %sub.24), calls=%async_computation.1 | async-start | bytes 8192 | tf_op jit(solution)/shard_map/all_to_all | solution.py:77
  119.7 9.9 %all-to-all-start = ((f32[8,1,3072]{2,1,0:T(1,128)}), f32[8,1,3072]{2,1,0:T(1,128)}, u32[]{:S(2)}, u32[]{:S(2)}) async-start(f32[8,1,3072]{2,1,0:T(1,128)} %reshape.725), calls=%async_computation | async-start | bytes 196608 | tf_op jit(solution)/shard_map/all_to_all | solution.py:106
  124.5 150.3 %all-reduce.4.cloned.1.call-start = ((), (), s32[]{:S(2)}) async-start(), calls=%async_computation.7 | async-start | bytes 524288 | tf_op jit(solution)/shard_map/psum | solution.py:110
  136.4 572.2 %all-reduce.6.cloned.1.call-start = ((), (), s32[]{:S(2)}) async-start(), calls=%async_computation.8 | async-start | bytes 524288 | tf_op jit(solution)/shard_map/psum | solution.py:110
  334.4 9.3 %collective-permute-start.19 = (f32[64,192]{1,0:T(8,128)S(1)}, f32[64,192]{1,0:T(8,128)}, u32[]{:S(2)}, u32[]{:S(2)}) collective-permute-start(f32[64,192]{1,0:T(8,128)S(1)} %get-tuple-element.31), channel_id=1, source_target_pairs={{16,0},{24,8},{32,16},{40,24},{48,32},{56,40},{64,48},{72,56},{80,... | collective-permute-start | bytes 147464 | tf_op jit(solution)/shard_map/ppermute | solution.py:16
  335.0 8.7 %collective-permute-start.18 = (f32[64,192]{1,0:T(8,128)S(1)}, f32[64,192]{1,0:T(8,128)}, u32[]{:S(2)}, u32[]{:S(2)}) collective-permute-start(f32[64,192]{1,0:T(8,128)S(1)} %get-tuple-element.32), channel_id=1, source_target_pairs={{240,0},{248,8},{0,16},{8,24},{16,32},{24,40},{32,48},{40,56},{48,... | collective-permute-start | bytes 147464 | tf_op jit(solution)/shard_map/ppermute | solution.py:16
  337.4 9.0 %collective-permute-start.17 = (f32[64,192]{1,0:T(8,128)S(1)}, f32[64,192]{1,0:T(8,128)}, u32[]{:S(2)}, u32[]{:S(2)}) collective-permute-start(f32[64,192]{1,0:T(8,128)S(1)} %get-tuple-element.33), channel_id=1, source_target_pairs={{8,0},{16,8},{24,16},{32,24},{40,32},{48,40},{56,48},{64,56},{72,6... | collective-permute-start | bytes 147464 | tf_op jit(solution)/shard_map/ppermute | solution.py:16
  340.1 20.3 %collective-permute-start.20 = (f32[64,192]{1,0:T(8,128)}, f32[64,192]{1,0:T(8,128)}, u32[]{:S(2)}, u32[]{:S(2)}) collective-permute-start(f32[64,192]{1,0:T(8,128)} %get-tuple-element.30), channel_id=1, source_target_pairs={{232,0},{240,8},{248,16},{0,24},{8,32},{16,40},{24,48},{32,56},{40... | collective-permute-start | bytes 147464 | tf_op jit(solution)/shard_map/ppermute | solution.py:16
  340.1 22.1 %collective-permute-start.21 = (f32[64,192]{1,0:T(8,128)}, f32[64,192]{1,0:T(8,128)}, u32[]{:S(2)}, u32[]{:S(2)}) collective-permute-start(f32[64,192]{1,0:T(8,128)} %get-tuple-element.29), channel_id=1, source_target_pairs={{24,0},{32,8},{40,16},{48,24},{56,32},{64,40},{72,48},{80,56},{88,... | collective-permute-start | bytes 147464 | tf_op jit(solution)/shard_map/ppermute | solution.py:16
  343.7 20.4 %collective-permute-start.22 = (f32[64,192]{1,0:T(8,128)}, f32[64,192]{1,0:T(8,128)}, u32[]{:S(2)}, u32[]{:S(2)}) collective-permute-start(f32[64,192]{1,0:T(8,128)} %get-tuple-element.28), channel_id=1, source_target_pairs={{224,0},{232,8},{240,16},{248,24},{0,32},{8,40},{16,48},{24,56},{3... | collective-permute-start | bytes 147464 | tf_op jit(solution)/shard_map/ppermute | solution.py:16
  343.7 22.2 %collective-permute-start.23 = (f32[64,192]{1,0:T(8,128)}, f32[64,192]{1,0:T(8,128)}, u32[]{:S(2)}, u32[]{:S(2)}) collective-permute-start(f32[64,192]{1,0:T(8,128)} %get-tuple-element.27), channel_id=1, source_target_pairs={{32,0},{40,8},{48,16},{56,24},{64,32},{72,40},{80,48},{88,56},{96,... | collective-permute-start | bytes 147464 | tf_op jit(solution)/shard_map/ppermute | solution.py:16
  346.4 21.3 %collective-permute-start.16 = (f32[64,192]{1,0:T(8,128)}, f32[64,192]{1,0:T(8,128)}, u32[]{:S(2)}, u32[]{:S(2)}) collective-permute-start(f32[64,192]{1,0:T(8,128)} %get-tuple-element.26), channel_id=1, source_target_pairs={{248,0},{0,8},{8,16},{16,24},{24,32},{32,40},{40,48},{48,56},{56,6... | collective-permute-start | bytes 147464 | tf_op jit(solution)/shard_map/ppermute | solution.py:16
  457.9 9.0 %collective-permute-start.27 = (f32[64,192]{1,0:T(8,128)S(1)}, f32[64,192]{1,0:T(8,128)S(1)}, u32[]{:S(2)}, u32[]{:S(2)}) collective-permute-start(f32[64,192]{1,0:T(8,128)S(1)} %get-tuple-element.23), channel_id=1, source_target_pairs={{16,0},{24,8},{32,16},{40,24},{48,32},{56,40},{64,48},{72,56},{80,... | collective-permute-start | bytes 147464 | tf_op jit(solution)/shard_map/ppermute | solution.py:16
  463.5 8.7 %collective-permute-start.29 = (f32[64,192]{1,0:T(8,128)}, f32[64,192]{1,0:T(8,128)}, u32[]{:S(2)}, u32[]{:S(2)}) collective-permute-start(f32[64,192]{1,0:T(8,128)} %get-tuple-element.21), channel_id=1, source_target_pairs={{24,0},{32,8},{40,16},{48,24},{56,32},{64,40},{72,48},{80,56},{88,... | collective-permute-start | bytes 147464 | tf_op jit(solution)/shard_map/ppermute | solution.py:16
  467.0 8.8 %collective-permute-start.31 = (f32[64,192]{1,0:T(8,128)}, f32[64,192]{1,0:T(8,128)}, u32[]{:S(2)}, u32[]{:S(2)}) collective-permute-start(f32[64,192]{1,0:T(8,128)} %get-tuple-element.19), channel_id=1, source_target_pairs={{32,0},{40,8},{48,16},{56,24},{64,32},{72,40},{80,48},{88,56},{96,... | collective-permute-start | bytes 147464 | tf_op jit(solution)/shard_map/ppermute | solution.py:16
  751.6 9.2 %collective-permute-start.35 = (f32[64,192]{1,0:T(8,128)S(1)}, f32[64,192]{1,0:T(8,128)S(1)}, u32[]{:S(2)}, u32[]{:S(2)}) collective-permute-start(f32[64,192]{1,0:T(8,128)S(1)} %get-tuple-element.15), channel_id=1, source_target_pairs={{16,0},{24,8},{32,16},{40,24},{48,32},{56,40},{64,48},{72,56},{80,... | collective-permute-start | bytes 147464 | tf_op jit(solution)/shard_map/ppermute | solution.py:16
  754.6 8.9 %collective-permute-start.33 = (f32[64,192]{1,0:T(8,128)S(1)}, f32[64,192]{1,0:T(8,128)S(1)}, u32[]{:S(2)}, u32[]{:S(2)}) collective-permute-start(f32[64,192]{1,0:T(8,128)S(1)} %get-tuple-element.17), channel_id=1, source_target_pairs={{8,0},{16,8},{24,16},{32,24},{40,32},{48,40},{56,48},{64,56},{72,6... | collective-permute-start | bytes 147464 | tf_op jit(solution)/shard_map/ppermute | solution.py:16
  757.2 8.7 %collective-permute-start.36 = (f32[64,192]{1,0:T(8,128)}, f32[64,192]{1,0:T(8,128)}, u32[]{:S(2)}, u32[]{:S(2)}) collective-permute-start(f32[64,192]{1,0:T(8,128)} %get-tuple-element.14), channel_id=1, source_target_pairs={{232,0},{240,8},{248,16},{0,24},{8,32},{16,40},{24,48},{32,56},{40... | collective-permute-start | bytes 147464 | tf_op jit(solution)/shard_map/ppermute | solution.py:16
  757.2 10.5 %collective-permute-start.37 = (f32[64,192]{1,0:T(8,128)}, f32[64,192]{1,0:T(8,128)}, u32[]{:S(2)}, u32[]{:S(2)}) collective-permute-start(f32[64,192]{1,0:T(8,128)} %get-tuple-element.13), channel_id=1, source_target_pairs={{24,0},{32,8},{40,16},{48,24},{56,32},{64,40},{72,48},{80,56},{88,... | collective-permute-start | bytes 147464 | tf_op jit(solution)/shard_map/ppermute | solution.py:16
  760.8 8.7 %collective-permute-start.38 = (f32[64,192]{1,0:T(8,128)S(1)}, f32[64,192]{1,0:T(8,128)}, u32[]{:S(2)}, u32[]{:S(2)}) collective-permute-start(f32[64,192]{1,0:T(8,128)S(1)} %get-tuple-element.12), channel_id=1, source_target_pairs={{224,0},{232,8},{240,16},{248,24},{0,32},{8,40},{16,48},{24,56},{3... | collective-permute-start | bytes 147464 | tf_op jit(solution)/shard_map/ppermute | solution.py:16
  760.8 10.5 %collective-permute-start.39 = (f32[64,192]{1,0:T(8,128)S(1)}, f32[64,192]{1,0:T(8,128)}, u32[]{:S(2)}, u32[]{:S(2)}) collective-permute-start(f32[64,192]{1,0:T(8,128)S(1)} %get-tuple-element.11), channel_id=1, source_target_pairs={{32,0},{40,8},{48,16},{56,24},{64,32},{72,40},{80,48},{88,56},{96,... | collective-permute-start | bytes 147464 | tf_op jit(solution)/shard_map/ppermute | solution.py:16
  763.5 9.6 %collective-permute-start.32 = (f32[64,192]{1,0:T(8,128)S(1)}, f32[64,192]{1,0:T(8,128)}, u32[]{:S(2)}, u32[]{:S(2)}) collective-permute-start(f32[64,192]{1,0:T(8,128)S(1)} %get-tuple-element.10), channel_id=1, source_target_pairs={{248,0},{0,8},{8,16},{16,24},{24,32},{32,40},{40,48},{48,56},{56,6... | collective-permute-start | bytes 147464 | tf_op jit(solution)/shard_map/ppermute | solution.py:16
  (67 other events, 2204.3 us)
Sparse Core Ops, SparseCore 0:
  136.6 138.1 all-reduce.3
  571.7 136.9 all-reduce.5
